TPU v7x, 32 devices: a whole 2x2x4 slice. The times are simulated.
32 devices in a mesh: ens: 2 (over y), space: 4 (over z), tm: 2 (over x), mom: 2 (over core).
Axes of the slice: x: 2, y: 2, z: 4, core: 2. Of those that a mesh axis runs over, the one named last changes fastest.
Arguments:
- eigvecs: bfloat16 [8, 2, 3, 256, 2048], P(('ens', 'tm'), None, None, None, 'space'), parts along dimension 0, may hold values from -0.359375 to 0.359375
- momenta: int32 [4, 3], P('mom'), may hold values from 1 to 2
- pairs: int32 [2, 2], replicated, may hold values from 0 to 3, as said below
- spin_weights: float32 [4, 4], replicated, may hold values from -1 to 1
- perambulators: bfloat16 [4, 2, 4, 4, 256, 256], P(('ens', 'tm'), None, None, None, 'space'), parts along dimension 0, may hold values from -0.0234375 to 0.0234375
Outputs:
- blocks: bfloat16 [4, 4, 2, 256, 256], P(('ens', 'tm'), 'mom', None, 'space'), parts along dimension 0
There are 2 independent parts, one for each index of `ens`. A program takes and returns all parts, laid end to end along the dimension named above; an argument that names none is the same for every part. Nothing has to cross between parts.
Inputs may be any that keep to these rules, and one draw needn't show every extreme that they name: pairs[q, 0], the sink, lies in time group q: (q) * 2 <= pairs[q, 0] < (q + 1) * 2; pairs[q, 1], the source, is any timeslice.
All inputs are finite; a program needn't handle non-finite values.
Results may differ from a plain program's by a relative error of at most 0.008.
Values may be sent and summed in bfloat16 or wider, within the bound.
No kernel may reach another device: no remote copies, remote signals or barrier semaphores. Data moves between devices by JAX's collectives and lax.ppermute only.
A program may use at most 64 MiB of HBM per device.

v0:
```python
import math
import jax
import jax.numpy as jnp
from jax import lax
from jax.sharding import PartitionSpec as P

LAT = 48
EXACT_PRECISION = lax.Precision.HIGHEST


def phases(momenta, site_ids):
    xcoord = (site_ids % LAT).astype(jnp.float32)
    ycoord = (site_ids // LAT % LAT).astype(jnp.float32)
    zcoord = (site_ids // (LAT * LAT)).astype(jnp.float32)
    mom_float = momenta.astype(jnp.float32)
    angles = (
        mom_float[:, 0:1] * xcoord + mom_float[:, 1:2] * ycoord + mom_float[:, 2:3] * zcoord
    ) * (2.0 * math.pi / LAT)
    return (jnp.cos(angles), jnp.sin(angles))


def elemental_terms(eigvecs, cosine_rows, sine_rows):
    contract_dims = (((0, 2), (0, 2)), ((), ()))
    per_time = []
    for which_time in range(eigvecs.shape[0]):
        real_vec = eigvecs[which_time, 0]
        imag_vec = eigvecs[which_time, 1]
        real_wide = real_vec.astype(jnp.float32)
        imag_wide = imag_vec.astype(jnp.float32)
        per_mom = []
        for which_mom in range(cosine_rows.shape[0]):
            cosine = cosine_rows[which_mom]
            sine = sine_rows[which_mom]
            real_turned = (cosine * real_wide + sine * imag_wide).astype(jnp.bfloat16)
            imag_turned = (cosine * imag_wide - sine * real_wide).astype(jnp.bfloat16)
            real_part = lax.dot_general(
                real_vec, real_turned, contract_dims, preferred_element_type=jnp.float32
            ) + lax.dot_general(
                imag_vec, imag_turned, contract_dims, preferred_element_type=jnp.float32
            )
            imag_part = lax.dot_general(
                real_vec, imag_turned, contract_dims, preferred_element_type=jnp.float32
            ) - lax.dot_general(
                imag_vec, real_turned, contract_dims, preferred_element_type=jnp.float32
            )
            per_mom.append(jnp.stack([real_part, imag_part]))
        per_time.append(jnp.stack(per_mom))
    return jnp.stack(per_time)


def source_slots(held_rows, pairs, my_group, times_dev, tm_size, pair_dev):
    wanted = pairs[:, 1].reshape(tm_size, pair_dev)
    local_times = jnp.arange(times_dev, dtype=jnp.int32) + my_group * times_dev
    chosen = (wanted[:, :, None] == local_times).astype(jnp.bfloat16)
    return jnp.einsum(
        "rqt,tmcij->rqmcij", chosen, held_rows, preferred_element_type=jnp.float32
    ).astype(jnp.bfloat16)


def sink_select(held_rows, my_pairs, my_group, times_dev):
    local_times = jnp.arange(times_dev, dtype=jnp.int32) + my_group * times_dev
    chosen = (my_pairs[:, 0][:, None] == local_times).astype(jnp.bfloat16)
    return jnp.einsum(
        "qt,tmcij->qmcij", chosen, held_rows, preferred_element_type=jnp.float32
    ).astype(jnp.bfloat16)


def bridge(mixed_block, source):
    real_part = jnp.einsum(
        "qkl,qmjl->qmkj", mixed_block[:, 0], source[:, :, 0], preferred_element_type=jnp.float32
    ) + jnp.einsum(
        "qkl,qmjl->qmkj", mixed_block[:, 1], source[:, :, 1], preferred_element_type=jnp.float32
    )
    imag_part = jnp.einsum(
        "qkl,qmjl->qmkj", mixed_block[:, 1], source[:, :, 0], preferred_element_type=jnp.float32
    ) - jnp.einsum(
        "qkl,qmjl->qmkj", mixed_block[:, 0], source[:, :, 1], preferred_element_type=jnp.float32
    )
    return jnp.stack([real_part, imag_part], 2).astype(jnp.bfloat16)


def attach(sink_elem, bridged):
    real_part = jnp.einsum(
        "qmik,qmkj->qmij", sink_elem[:, :, 0], bridged[:, :, 0], preferred_element_type=jnp.float32
    ) - jnp.einsum(
        "qmik,qmkj->qmij", sink_elem[:, :, 1], bridged[:, :, 1], preferred_element_type=jnp.float32
    )
    imag_part = jnp.einsum(
        "qmik,qmkj->qmij", sink_elem[:, :, 0], bridged[:, :, 1], preferred_element_type=jnp.float32
    ) + jnp.einsum(
        "qmik,qmkj->qmij", sink_elem[:, :, 1], bridged[:, :, 0], preferred_element_type=jnp.float32
    )
    return jnp.stack([real_part, imag_part], 2)


def local(eigvecs, momenta, pairs, spin_weights, perambulators):
    times_dev = eigvecs.shape[0]
    vec_count = eigvecs.shape[3]
    sites_dev = eigvecs.shape[4]
    pair_dev = perambulators.shape[0]
    tm_size = lax.axis_size("tm")
    space_size = lax.axis_size("space")
    my_group = lax.axis_index("tm")
    my_place = lax.axis_index("space")
    rows_dev = vec_count // space_size
    row_first = my_place * rows_dev
    site_ids = my_place * sites_dev + jnp.arange(sites_dev, dtype=jnp.int32)
    cosine_rows, sine_rows = phases(momenta, site_ids)
    partial_value = elemental_terms(eigvecs, cosine_rows, sine_rows)
    my_pairs = lax.dynamic_slice_in_dim(pairs, my_group * pair_dev, pair_dev, 0)
    whole = lax.psum(partial_value, "space").astype(jnp.bfloat16)
    outgoing = source_slots(whole, pairs, my_group, times_dev, tm_size, pair_dev)
    arrived = lax.all_to_all(outgoing, "tm", split_axis=0, concat_axis=0, tiled=True)
    source_full = jnp.sum(arrived, axis=0, dtype=jnp.float32).astype(jnp.bfloat16)
    sink_whole = sink_select(whole, my_pairs, my_group, times_dev)
    sink_own = lax.dynamic_slice_in_dim(sink_whole, row_first, rows_dev, 3)
    mixed_peramb = jnp.einsum(
        "ab,qcabkl->qckl",
        spin_weights,
        perambulators.astype(jnp.float32),
        precision=EXACT_PRECISION,
    ).astype(jnp.bfloat16)
    bridged = bridge(lax.all_gather(mixed_peramb, "space", axis=2, tiled=True), source_full)
    blocks = attach(sink_own, bridged).astype(jnp.bfloat16)
    return blocks


def solution(mesh):
    return jax.shard_map(
        local,
        mesh=mesh,
        in_specs=(
            P(("ens", "tm"), None, None, None, "space"),
            P("mom", None),
            P(),
            P(),
            P(("ens", "tm"), None, None, None, "space", None),
        ),
        out_specs=P(("ens", "tm"), "mom", None, "space", None),
        check_vma=False,
    )
```

profile of v0, /device:TPU:0, one launch (start us, length us, event | category | flops | bytes accessed | tf_op | source)
XLA Modules:
  0.0 120.1 jit_solution(8111220607492806430)
XLA Ops:
  0.0 0.0 copy-start
  0.0 0.8 convert_element_type.166
  0.8 0.2 slice_reduce_fusion.3
  1.0 0.1 fusion.149
  1.1 0.1 sin.3
  1.3 0.0 copy-start.1
  1.3 2.2 %convolution_bitcast_fusion.14 = f32[256,256]{1,0:T(8,128)S(1)} fusion(f32[512]{0:T(512)S(1)} %bitcast.288, f32[512]{0:T(512)S(1)} %bitcast.296, bf16[2,2,3,256,512]{4,3,2,1,0:T(8,128)(2,1)} %param.5), kind=kOutput, calls=%fused_computation.55 | convolution fusion | flops 203685888 | bytes 2625536 | tf_op jit(solution)/shard_map/dot_general | solution.py:38
  3.5 0.4 copy-done.1
  3.9 0.4 convolution_bitcast_fusion.12
  4.3 0.5 convolution_bitcast_fusion.10
  4.8 0.4 convolution_bitcast_fusion.8
  5.2 0.4 convolution_bitcast_fusion.6
  5.7 0.5 convolution_bitcast_fusion.4
  6.1 0.5 convolution_bitcast_fusion.2
  6.6 0.4 convolution_bitcast_fusion
  7.1 0.4 fusion.22
  7.5 0.5 fusion.24
  8.0 0.5 fusion.26
  8.4 0.5 fusion.28
  8.9 0.5 fusion.30
  9.4 0.5 fusion.32
  9.8 0.5 fusion.34
  10.3 0.5 fusion.36
  10.8 0.1 maximum_bitcast_fusion
  11.0 0.1 maximum_bitcast_fusion.1
  11.1 0.1 pad_maximum_fusion
  11.2 79.3 %all-reduce.1 = bf16[2,2,2,256,256]{3,4,2,1,0:T(8,128)(2,1)} all-reduce(f32[2,2,2,256,256]{3,4,2,1,0:T(8,128)S(1)} %pad_maximum_fusion), channel_id=1, replica_groups=mesh['ens'=2,'space'=4,'tm'=2,'mom'=2] {'space'}, use_global_device_ids=true, to_apply=%region_0.1 | all-reduce | flops 524288 | bytes 3145728 | tf_op jit(solution)/shard_map/psum | solution.py:111
  90.5 2.5 %copy.12 = bf16[2,2,2,256,256]{4,0,3,2,1:T(2,128)(2,1)S(1)} copy(bf16[2,2,2,256,256]{3,4,2,1,0:T(8,128)(2,1)} %all-reduce.1) | data formatting | bytes 2097152 | tf_op jit(solution)/shard_map/convert_element_type | solution.py:111
  93.1 0.0 copy-done.3
  93.1 0.2 slice_reduce_fusion
  93.3 1.3 %fusion.16 = bf16[2,1,2,2,256,256]{5,0,4,3,2,1:T(2,128)(2,1)S(1)} fusion(bf16[2,2,2,256,256]{4,0,3,2,1:T(2,128)(2,1)S(1)} %copy.12, s32[2]{0:T(128)S(1)} %iota_add_fusion.1, s32[2]{0:T(128)S(1)} %slice_reduce_fusion), kind=kOutput, calls=%fused_computation.34 | convolution fusion | flops 2621444 | bytes 2097168 | tf_op jit(solution)/shard_map/rqt,tmcij->rqmcij/dot_general | solution.py:55
  94.6 1.1 copy.13
  95.7 3.9 %all-to-all-start = ((bf16[2,1,2,2,256,256]{5,4,3,2,1,0:T(8,128)(2,1)}), bf16[2,1,2,2,256,256]{5,4,3,2,1,0:T(8,128)(2,1)S(1)}, u32[]{:S(2)}, u32[]{:S(2)}) async-start(bf16[2,1,2,2,256,256]{5,4,3,2,1,0:T(8,128)(2,1)} %copy.13), calls=%async_computation | async-start | bytes 2097152 | tf_op jit(solution)/shard_map/all_to_all | solution.py:113
  99.6 2.1 %fusion.41 = bf16[1,2,64,256,1]{3,0,4,2,1:T(2,128)(2,1)S(1)} fusion(f32[4,4,1,1,1]{1,2,0,4,3:T(1,128)S(1)} %bitcast.304, bf16[2,4,4,64,256]{4,3,2,1,0:T(8,128)(2,1)S(1)} %bitcast.261), kind=kOutput, calls=%fused_computation.82 | convolution fusion | flops 6291456 | bytes 1114176 | tf_op jit(solution)/shard_map/ab,qcabkl->qckl/dot_general | solution.py:117
  101.8 1.3 %fusion.145 = bf16[1,2,2,256,256]{4,0,3,2,1:T(2,128)(2,1)S(1)} fusion(bf16[2,2,2,256,256]{4,0,3,2,1:T(2,128)(2,1)S(1)} %copy.12, s32[]{:T(128)S(1)} %bitcast.305, s32[]{:T(128)S(6)} %mul.205), kind=kOutput, calls=%fused_computation.194 | convolution fusion | flops 1048580 | bytes 1572872 | tf_op jit(solution)/shard_map/qt,tmcij->qmcij/dot_general | solution.py:63
  103.0 0.1 copy.37
  103.1 13.8 %all-gather = bf16[2,256,256]{2,1,0:T(8,128)(2,1)S(1)} all-gather(bf16[2,64,256]{2,1,0:T(8,128)(2,1)S(1)} %bitcast.271), channel_id=2, replica_groups=mesh['ens'=2,'space'=4,'tm'=2,'mom'=2] {'space'}, dimensions={1}, use_global_device_ids=true | all-gather | bytes 327680 | tf_op jit(solution)/shard_map/all_gather | solution.py:123
  116.9 0.0 all-to-all-done
  116.9 0.5 reduce_sum.14
  117.5 0.2 fusion.100
  117.7 0.3 fusion.99
  118.0 0.3 fusion.20
  118.3 0.3 fusion.19
  118.5 0.2 fusion.135
  118.7 0.2 fusion.134
  118.9 0.2 fusion.40
  119.2 0.2 fusion.39
  119.4 0.7 copy.20
  (18 shorter events, 0.3 us)
Async XLA Ops:
  0.0 99.6 %copy-start = (bf16[1,2,4,4,64,256]{5,4,3,2,1,0:T(8,128)(2,1)S(1)}, bf16[1,2,4,4,64,256]{5,4,3,2,1,0:T(8,128)(2,1)}, u32[]{:S(2)}) copy-start(bf16[1,2,4,4,64,256]{5,4,3,2,1,0:T(8,128)(2,1)} %param.9) | copy-start | bytes 3145732
  1.3 2.6 %copy-start.1 = (bf16[2,2,3,256,512]{4,3,2,1,0:T(8,128)(2,1)S(1)}, bf16[2,2,3,256,512]{4,3,2,1,0:T(8,128)(2,1)}, u32[]{:S(2)}) copy-start(bf16[2,2,3,256,512]{4,3,2,1,0:T(8,128)(2,1)} %param.5) | copy-start | bytes 9437188
  90.5 2.6 %copy-start.3 = (s32[2,2]{1,0:T(2,128)S(1)}, s32[2,2]{1,0:T(2,128)}, u32[]{:S(2)}) copy-start(s32[2,2]{1,0:T(2,128)} %param.7) | copy-start | bytes 52
  95.7 3.9 %copy-start.2 = (f32[4,4]{1,0:T(4,128)S(1)}, f32[4,4]{1,0:T(4,128)}, u32[]{:S(2)}) copy-start(f32[4,4]{1,0:T(4,128)} %param.8) | copy-start | bytes 196
  95.7 21.2 %all-to-all-start = ((bf16[2,1,2,2,256,256]{5,4,3,2,1,0:T(8,128)(2,1)}), bf16[2,1,2,2,256,256]{5,4,3,2,1,0:T(8,128)(2,1)S(1)}, u32[]{:S(2)}, u32[]{:S(2)}) async-start(bf16[2,1,2,2,256,256]{5,4,3,2,1,0:T(8,128)(2,1)} %copy.13), calls=%async_computation | async-start | bytes 2097152 | tf_op jit(solution)/shard_map/all_to_all | solution.py:113
where the time goes:
time: 120 us
  blocking collectives  93.1 us (78%)
  matrix products  15.5 us (13%)
  local copies, waits for them, and re-layouts  5.32 us (4%)
  starting transfers between devices  3.89 us (3%)
  other arithmetic  1.86 us (2%)
    psum x1, blocking collectives, local(): whole = lax.psum(partial_value, 'space').astype(jnp.bfloat16)  79.3 us
    all_gather x1, blocking collectives, local(): lax.all_gather(mixed_peramb, 'space', axis=2, tiled=True)  13.8 us
    all_to_all x1, starting transfers between devices, local(): lax.all_to_all(outgoing, 'tm', split_axis=0, concat_axis=0, tiled=True)  3.89 us
    dot_general x4, matrix products, elemental_terms(): lax.dot_general(imag_vec, imag_turned, contract_dims, preferred_element_t...  3.57 us
    convert_element_type x1, local copies, waits for them, and re-layouts, local(): whole = lax.psum(partial_value, 'space').astype(jnp.bfloat16)  2.54 us
  transfers between devices with their start and end apart: 1, of which 0 were waited for; matrix products, arithmetic and copies ran while one was open for 3% of the time, Pallas kernels for 0%

commit v1 on v0

--- a/solution.py
+++ b/solution.py
@@ -108,7 +108,8 @@
     cosine_rows, sine_rows = phases(momenta, site_ids)
     partial_value = elemental_terms(eigvecs, cosine_rows, sine_rows)
     my_pairs = lax.dynamic_slice_in_dim(pairs, my_group * pair_dev, pair_dev, 0)
-    whole = lax.psum(partial_value, "space").astype(jnp.bfloat16)
+    refer_words_for = lambda sample, group_axis: jnp.sum(lax.all_gather(sample, group_axis), axis=0)
+    whole = refer_words_for(partial_value, "space").astype(jnp.bfloat16)
     outgoing = source_slots(whole, pairs, my_group, times_dev, tm_size, pair_dev)
     arrived = lax.all_to_all(outgoing, "tm", split_axis=0, concat_axis=0, tiled=True)
     source_full = jnp.sum(arrived, axis=0, dtype=jnp.float32).astype(jnp.bfloat16)

time: 120 us -> 210 us (1.75)
  waiting for transfers between devices: 0.01 us -> 150 us
  blocking collectives: 93.1 us -> 14.3 us
  between operations: 0.38 us -> 13.8 us
  other arithmetic: 1.86 us -> 6.05 us
    all_gather x0 -> x1, waiting for transfers between devices: none -> 150 us  [local(): lax.all_gather(sample, group_axis)]
    psum x1 -> x0, blocking collectives: 79.3 us -> none  [local(): whole = lax.psum(partial_value, 'space').astype(jnp.bfloat16)]
    reduce_sum x0 -> x1, other arithmetic: none -> 4.19 us  [local(): jnp.sum(lax.all_gather(sample, group_axis), axis=0)]
  transfers between devices with their start and end apart: 1 -> 2, of which waited for: 0 -> 1; matrix products, arithmetic and copies ran while one was open for 3% -> 2% of each run, Pallas kernels for 0% -> 0%
where the time goes in v1:
time: 210 us
  waiting for transfers between devices  150 us (71%)
  matrix products  15.5 us (7%)
  blocking collectives  14.3 us (7%)
  between operations  13.8 us (7%)
  local copies, waits for them, and re-layouts  6.89 us (3%)
  other arithmetic  6.05 us (3%)
  starting transfers between devices  3.71 us (2%)
    all_gather x1, waiting for transfers between devices, local(): lax.all_gather(sample, group_axis)  150 us
    all_gather x1, blocking collectives, local(): lax.all_gather(mixed_peramb, 'space', axis=2, tiled=True)  14.3 us
  transfers between devices with their start and end apart: 2, of which 1 were waited for; matrix products, arithmetic and copies ran while one was open for 2% of the time, Pallas kernels for 0%

profile of v1, /device:TPU:0, one launch (start us, length us, event | category | flops | bytes accessed | tf_op | source)
XLA Modules:
  0.0 209.8 jit_solution(2841178052176012010)
XLA Ops:
  6.6 0.8 convert_element_type.166
  7.3 0.2 slice_reduce_fusion.3
  7.5 0.1 fusion.149
  7.7 0.1 sin.3
  7.8 2.2 %convolution_bitcast_fusion.14 = f32[256,256]{1,0:T(8,128)S(1)} fusion(f32[512]{0:T(512)S(1)} %bitcast.290, f32[512]{0:T(512)S(1)} %bitcast.298, bf16[2,2,3,256,512]{4,3,2,1,0:T(8,128)(2,1)} %param.5), kind=kOutput, calls=%fused_computation.55 | convolution fusion | flops 203685888 | bytes 2625536 | tf_op jit(solution)/shard_map/dot_general | solution.py:38
  10.0 0.4 copy-done.3
  10.4 0.4 convolution_bitcast_fusion.12
  10.8 0.5 convolution_bitcast_fusion.10
  11.3 0.4 convolution_bitcast_fusion.8
  11.8 0.5 convolution_bitcast_fusion.6
  12.2 0.5 convolution_bitcast_fusion.4
  12.7 0.5 convolution_bitcast_fusion.2
  13.1 0.4 convolution_bitcast_fusion
  13.6 0.4 fusion.22
  14.0 0.5 fusion.24
  14.5 0.5 fusion.26
  15.0 0.5 fusion.28
  15.4 0.5 fusion.30
  15.9 0.5 fusion.32
  16.4 0.5 fusion.34
  16.8 0.5 fusion.36
  17.4 0.1 maximum_bitcast_fusion
  17.5 0.1 maximum_bitcast_fusion.1
  17.6 0.1 pad_maximum_fusion
  17.8 2.1 copy.11
  19.9 0.6 copy-done.4
  20.5 2.1 %fusion.41 = bf16[1,2,64,256,1]{3,0,4,2,1:T(2,128)(2,1)S(1)} fusion(f32[4,4,1,1,1]{1,2,0,4,3:T(1,128)S(1)} %bitcast.306, bf16[2,4,4,64,256]{4,3,2,1,0:T(8,128)(2,1)S(1)} %bitcast.262), kind=kOutput, calls=%fused_computation.82 | convolution fusion | flops 6291456 | bytes 1114176 | tf_op jit(solution)/shard_map/ab,qcabkl->qckl/dot_general | solution.py:118
  22.7 0.2 slice_reduce_fusion
  22.8 149.5 %all-gather.4.cloned.1.call-done = f32[8,2,2,256,256]{4,3,2,1,0:T(8,128)} async-done(((f32[2,2,2,256,256]{4,3,2,1,0:T(8,128)}), f32[8,2,2,256,256]{4,3,2,1,0:T(8,128)}) %all-gather.4.cloned.1.call-update) | async-done | bytes 8388624 | tf_op jit(solution)/shard_map/all_gather | solution.py:111
  172.3 4.2 %reduce_sum.23 = bf16[2,2,2,256,256]{4,3,2,1,0:T(8,128)(2,1)S(1)} reduce(f32[4,2,2,2,256,256]{5,4,3,2,1,0:T(8,128)} %bitcast.263, f32[]{:T(128)} %constant.49.clone.1), dimensions={0}, to_apply=%region_0.1 | reduce | flops 1572864 | bytes 9437188 | tf_op jit(solution)/shard_map/reduce_sum | solution.py:111
  176.5 0.5 copy.32
  177.1 0.9 copy.13
  178.0 1.3 fusion.16
  179.3 1.1 copy.14
  180.4 3.7 %all-to-all-start = ((bf16[2,1,2,2,256,256]{5,4,3,2,1,0:T(8,128)(2,1)}), bf16[2,1,2,2,256,256]{5,4,3,2,1,0:T(8,128)(2,1)S(1)}, u32[]{:S(2)}, u32[]{:S(2)}) async-start(bf16[2,1,2,2,256,256]{5,4,3,2,1,0:T(8,128)(2,1)} %copy.14), calls=%async_computation | async-start | bytes 2097152 | tf_op jit(solution)/shard_map/all_to_all | solution.py:114
  184.1 14.3 %all-gather.1 = bf16[2,256,256]{2,1,0:T(8,128)(2,1)S(1)} all-gather(bf16[2,64,256]{2,1,0:T(8,128)(2,1)S(1)} %bitcast.273), channel_id=3, replica_groups=mesh['ens'=2,'space'=4,'tm'=2,'mom'=2] {'space'}, dimensions={1}, use_global_device_ids=true | all-gather | bytes 327680 | tf_op jit(solution)/shard_map/all_gather | solution.py:124
  198.5 1.3 fusion.145
  199.7 0.1 copy.39
  199.9 0.5 reduce_sum.24
  200.4 0.2 fusion.100
  200.6 0.3 fusion.99
  200.9 0.3 fusion.20
  201.2 0.3 fusion.19
  201.5 0.2 fusion.135
  201.7 0.2 fusion.134
  201.9 0.2 fusion.40
  202.1 0.2 fusion.39
  202.3 0.7 copy.21
  (27 shorter events, 0.3 us)
Async XLA Ops:
  6.5 13.3 %copy-start = (bf16[1,2,4,4,64,256]{5,4,3,2,1,0:T(8,128)(2,1)S(1)}, bf16[1,2,4,4,64,256]{5,4,3,2,1,0:T(8,128)(2,1)}, u32[]{:S(2)}) copy-start(bf16[1,2,4,4,64,256]{5,4,3,2,1,0:T(8,128)(2,1)} %param.9) | copy-start | bytes 3145732
  6.5 165.8 %all-gather.4.cloned.1.call-start = ((), (), s32[]{:S(2)}) async-start(), calls=%async_computation.1 | async-start | bytes 10485760 | tf_op jit(solution)/shard_map/all_gather | solution.py:111
  7.8 2.6 %copy-start.3 = (bf16[2,2,3,256,512]{4,3,2,1,0:T(8,128)(2,1)S(1)}, bf16[2,2,3,256,512]{4,3,2,1,0:T(8,128)(2,1)}, u32[]{:S(2)}) copy-start(bf16[2,2,3,256,512]{4,3,2,1,0:T(8,128)(2,1)} %param.5) | copy-start | bytes 9437188
  19.8 0.7 copy-start.4
  19.9 2.8 %copy-start.5 = (s32[2,2]{1,0:T(2,128)S(1)}, s32[2,2]{1,0:T(2,128)}, u32[]{:S(2)}) copy-start(s32[2,2]{1,0:T(2,128)} %param.7) | copy-start | bytes 52
  178.0 1.3 copy-start.1
  180.4 18.0 %copy-start.2 = (bf16[2,2,2,256,256]{4,0,3,2,1:T(2,128)(2,1)S(1)}, bf16[2,2,2,256,256]{4,0,3,2,1:T(2,128)(2,1)}, u32[]{:S(2)}) copy-start(bf16[2,2,2,256,256]{4,0,3,2,1:T(2,128)(2,1)} %copy-done.1) | copy-start | bytes 3145732
  180.4 19.4 %all-to-all-start = ((bf16[2,1,2,2,256,256]{5,4,3,2,1,0:T(8,128)(2,1)}), bf16[2,1,2,2,256,256]{5,4,3,2,1,0:T(8,128)(2,1)S(1)}, u32[]{:S(2)}, u32[]{:S(2)}) async-start(bf16[2,1,2,2,256,256]{5,4,3,2,1,0:T(8,128)(2,1)} %copy.14), calls=%async_computation | async-start | bytes 2097152 | tf_op jit(solution)/shard_map/all_to_all | solution.py:114
Sparse Core Ops, SparseCore 0:
  20.0 152.3 all-gather.3
